TPU v7x, 32 devices: a whole 2x2x4 slice. The times are simulated.
32 devices in a mesh: leaf: 16 (over z, y, x), sub: 2 (over core).
Axes of the slice: x: 2, y: 2, z: 4, core: 2. Of those that a mesh axis runs over, the one named last changes fastest.
Arguments:
- probes: float32 [64, 32768], P(None, ('leaf', 'sub')), may hold values from -600 to 600
- points: float32 [3, 32768], P(None, ('leaf', 'sub')), may hold values from -4 to 4
- leaf_order: int32 [32768], P(('leaf', 'sub')), may hold values from 0 to 1023, as said below
- near_list: int32 [64, 4], P(('leaf', 'sub')), may hold values from 0 to 63, as said below
- far_leaf_list: int32 [64, 2], P(('leaf', 'sub')), may hold values from 0 to 63, as said below
- far_chip_list: int32 [16, 8], P('leaf'), may hold values from -1 to 15, as said below
- leaf_basis: float32 [64, 512, 256], P(('leaf', 'sub')), may hold values from -0.25 to 0.25
- transfer: float32 [64, 256, 256], P(('leaf', 'sub')), may hold values from -0.1875 to 0.1875
- far_leaf_blocks: float32 [128, 256, 256], P(('leaf', 'sub')), may hold values from -0.25 to 0.25
- far_chip_blocks: float32 [128, 256, 256], P('leaf'), may hold values from -0.125 to 0.125
Outputs:
- result: float32 [64, 32768], P(None, ('leaf', 'sub'))
Inputs may be any that keep to these rules, and one draw needn't show every extreme that they name: `leaf_order`: each device's block of 1024 consecutive entries is a permutation of 0 to 1023. `near_list`: row l lists 4 distinct leaves, l among them, all held by the devices l // 2 - 1 to l // 2 + 1 of the joined axis leaf+sub, counted around the cycle. `far_leaf_list`: row l lists the 2 leaves of those same three devices that row l of near_list leaves out. `far_chip_list`: row k lists distinct chip clusters at cycle distance 2 to 5 from k, one to 8 of them, the used entries first and -1 in the rest; some row uses all 8.
All inputs are finite; a program needn't handle non-finite values.
Results may differ from a plain program's by a relative error of at most 0.0003.
Values sent between devices are 32-bit elements; how exact they have to be, the bound alone decides.
No kernel may reach another device: no remote copies, remote signals or barrier semaphores. Data moves between devices by JAX's collectives and lax.ppermute only.
A program may use at most 64 MiB of HBM per device.

v0:
```python
import jax
import jax.numpy as jnp
from jax import lax
from jax.sharding import PartitionSpec as P

CHIP_SPAN = 4
highest = lax.Precision.HIGHEST
inverse_width = 0.5 / (0.15 * 0.15)
epsilon = 1e-06


def from_behind(block, axis, distance):
    devices = range(lax.axis_size(axis))
    route = [((i - distance) % len(devices), i) for i in devices]
    return lax.ppermute(block, axis, route)


def kernel_tiles(source_points, target_points):
    spread = source_points[0] - target_points[0]
    distance = spread * spread
    for coord_axis in (1, 2):
        spread = source_points[coord_axis] - target_points[coord_axis]
        distance = distance + spread * spread
    return jnp.exp(-inverse_width * distance)


def leaf_window(values):
    pieces = []
    for offset in (1, 0, -1):
        if offset == 0:
            pieces.append(values)
        else:
            pieces.append(from_behind(values, ("leaf", "sub"), offset))
    first_device = lax.axis_index(("leaf", "sub")) - 1
    return (jnp.concatenate(pieces, 1), first_device)


def couple_chips(stacked, slot_place, used_count, far_chip_blocks):

    def add_slot(slot_index, running):
        source = stacked[slot_place[slot_index]]
        return running + jnp.dot(
            source,
            far_chip_blocks[slot_index],
            precision=highest,
            preferred_element_type=jnp.float32,
        )

    start_value = jnp.zeros((stacked.shape[1], stacked.shape[2]), jnp.float32)
    return lax.fori_loop(0, used_count, add_slot, start_value)


def chip_level(upward, far_chip_list, far_chip_blocks):
    chip_count = lax.axis_size("leaf")
    chip_index = lax.axis_index("leaf")
    slot_ids = far_chip_list[0]
    used_count = jnp.sum((slot_ids >= 0).astype(jnp.int32))
    offsets = jnp.mod(slot_ids - chip_index, chip_count)
    slot_place = jnp.where(
        offsets <= CHIP_SPAN + 1, offsets - 2, CHIP_SPAN + chip_count - offsets - 2
    )
    slot_place = jnp.clip(slot_place, 0, 2 * CHIP_SPAN - 1)
    shift_list = [-distance for distance in range(2, CHIP_SPAN + 2)] + [
        distance for distance in range(2, CHIP_SPAN + 2)
    ]
    halves = lax.psum_scatter(upward, "sub", scatter_dimension=0, tiled=True)
    pieces = [from_behind(halves, "leaf", offset) for offset in shift_list]
    coupled_half = couple_chips(jnp.stack(pieces), slot_place, used_count, far_chip_blocks)
    coupled = lax.all_gather(coupled_half, "sub", axis=0, tiled=True)
    return coupled


def apply_matrix(
    sorted_values,
    kernels,
    near_index,
    leaf_basis,
    transfer,
    far_leaf_list,
    far_leaf_blocks,
    far_chip_list,
    far_chip_blocks,
    leaf_total,
):
    columns = sorted_values.shape[0]
    leaf_count, leaf_size, rank_size = leaf_basis.shape
    value_window, window_start = leaf_window(sorted_values)
    window_tiles = value_window.reshape(columns, -1, leaf_size)
    source_values = jnp.take(window_tiles, near_index, axis=1)
    near_part = jnp.einsum("clnp,lnpq->clq", source_values, kernels, precision=highest)
    own_tiles = sorted_values.reshape(columns, leaf_count, leaf_size)
    coefficients = jnp.einsum("clp,lpr->lcr", own_tiles, leaf_basis, precision=highest)
    pieces = []
    for offset in (1, 0, -1):
        if offset == 0:
            pieces.append(coefficients)
        else:
            pieces.append(from_behind(coefficients, ("leaf", "sub"), offset))
    coeff_stack = jnp.concatenate(pieces, 0)
    device_index = lax.axis_index(("leaf", "sub"))
    far_index = jnp.mod(far_leaf_list - (device_index - 1) * leaf_count, leaf_total)
    far_sources = jnp.take(coeff_stack, far_index.reshape(-1), axis=0).reshape(
        leaf_count, -1, columns, rank_size
    )
    leaf_blocks = far_leaf_blocks.reshape(leaf_count, -1, rank_size, rank_size)
    local_far = jnp.einsum("ljcr,ljrs->lcs", far_sources, leaf_blocks, precision=highest)
    upward = jnp.einsum("lcr,lrs->cs", coefficients, transfer, precision=highest)
    chip_part = chip_level(upward, far_chip_list, far_chip_blocks)
    downward = local_far + jnp.einsum("cs,lrs->lcr", chip_part, transfer, precision=highest)
    far_part = jnp.einsum("lcr,lpr->clp", downward, leaf_basis, precision=highest)
    return (near_part + far_part).reshape(columns, leaf_count * leaf_size)


def on_device(
    probes,
    points,
    leaf_order,
    near_list,
    far_leaf_list,
    far_chip_list,
    leaf_basis,
    transfer,
    far_leaf_blocks,
    far_chip_blocks,
):
    leaf_count, leaf_size, rank_size = leaf_basis.shape
    leaf_total = leaf_count * lax.axis_size(("leaf", "sub"))
    point_total = probes.shape[1] * lax.axis_size(("leaf", "sub"))
    sorted_probes = probes[:, leaf_order]
    sorted_points = points[:, leaf_order]
    point_window, first_device = leaf_window(sorted_points)
    near_index = jnp.mod(near_list - first_device * leaf_count, leaf_total)
    point_tiles = point_window.reshape(3, -1, leaf_size)
    source_points = jnp.take(point_tiles, near_index, axis=1)
    target_points = sorted_points.reshape(3, leaf_count, leaf_size)
    kernels = kernel_tiles(source_points[..., :, None], target_points[:, :, None, None, :])
    first_pass = apply_matrix(
        sorted_probes,
        kernels,
        near_index,
        leaf_basis,
        transfer,
        far_leaf_list,
        far_leaf_blocks,
        far_chip_list,
        far_chip_blocks,
        leaf_total,
    )
    squares = lax.psum(jnp.sum(first_pass * first_pass, axis=1), ("leaf", "sub"))
    column_scale = lax.rsqrt(squares / point_total + epsilon)
    second = apply_matrix(
        first_pass * column_scale[:, None],
        kernels,
        near_index,
        leaf_basis,
        transfer,
        far_leaf_list,
        far_leaf_blocks,
        far_chip_list,
        far_chip_blocks,
        leaf_total,
    )
    return jnp.zeros_like(second).at[:, leaf_order].set(second)


def solution(mesh):
    return jax.shard_map(
        on_device,
        mesh=mesh,
        in_specs=(
            P(None, ("leaf", "sub")),
            P(None, ("leaf", "sub")),
            P(("leaf", "sub")),
            P(("leaf", "sub"), None),
            P(("leaf", "sub"), None),
            P("leaf", None),
            P(("leaf", "sub"), None, None),
            P(("leaf", "sub"), None, None),
            P(("leaf", "sub"), None, None),
            P("leaf", None, None),
        ),
        out_specs=P(None, ("leaf", "sub")),
        check_vma=False,
    )
```

profile of v0, /device:TPU:5, one launch (start us, length us, event | category | flops | bytes accessed | tf_op | source)
XLA Modules:
  0.0 316.3 jit_solution(15570008534534858504)
XLA Ops:
  6.5 1.4 broadcast_clamp_fusion
  9.1 4.0 %gather_fusion.2 = f32[1024,64]{1,0:T(8,128)} fusion(f32[64,1024]{0,1:T(8,128)S(1)} %copy.43, s32[1024]{0:T(1024)S(1)} %get-tuple-element.107), kind=kCustom, calls=%fused_computation.6 | custom fusion | bytes 528384 | tf_op jit(solution)/shard_map/gather | solution.py:129
  13.1 2.1 fusion.58
  17.1 1.8 copy.39
  18.9 3.8 %gather_fusion = f32[1024,3]{1,0:T(8,128)S(1)} fusion(f32[3,1024]{0,1:T(8,128)} %copy.39, s32[1024]{0:T(1024)S(1)} %get-tuple-element.107), kind=kCustom, calls=%fused_computation.4 | custom fusion | bytes 28672 | tf_op jit(solution)/shard_map/gather | solution.py:130
  22.8 1.7 collective-permute-start
  28.2 1.4 slice_reduce_fusion.2
  37.8 1.8 copy.42
  45.1 5.9 %collective-permute-start.6 = (f32[32,256]{1,0:T(8,128)}, f32[32,256]{1,0:T(8,128)S(1)}, u32[]{:S(2)}, u32[]{:S(2)}) collective-permute-start(f32[32,256]{1,0:T(8,128)} %reduce-scatter.3.cloned.1.call-done), channel_id=1, source_target_pairs={{4,0},{6,2},{8,4},{10,6},{12,8},{14,10},{16,12},{18,14},{20,16},{2... | collective-permute-start | bytes 98312 | tf_op jit(solution)/shard_map/ppermute | solution.py:15
  51.8 1.8 collective-permute-start.13
  54.9 10.9 %collective-permute-start.7 = (f32[32,256]{1,0:T(8,128)}, f32[32,256]{1,0:T(8,128)S(1)}, u32[]{:S(2)}, u32[]{:S(2)}) collective-permute-start(f32[32,256]{1,0:T(8,128)} %reduce-scatter.3.cloned.1.call-done), channel_id=1, source_target_pairs={{6,0},{8,2},{10,4},{12,6},{14,8},{16,10},{18,12},{20,14},{22,16},{... | collective-permute-start | bytes 98312 | tf_op jit(solution)/shard_map/ppermute | solution.py:15
  65.8 1.3 collective-permute-done.7
  67.3 3.2 %collective-permute-done.8 = f32[32,256]{1,0:T(8,128)S(1)} collective-permute-done((f32[32,256]{1,0:T(8,128)}, f32[32,256]{1,0:T(8,128)S(1)}, u32[]{:S(2)}, u32[]{:S(2)}) %collective-permute-start.8) | collective-permute-done | bytes 32800 | tf_op jit(solution)/shard_map/ppermute | solution.py:15
  70.6 5.1 %collective-permute-start.9 = (f32[32,256]{1,0:T(8,128)}, f32[32,256]{1,0:T(8,128)S(1)}, u32[]{:S(2)}, u32[]{:S(2)}) collective-permute-start(f32[32,256]{1,0:T(8,128)} %reduce-scatter.3.cloned.1.call-done), channel_id=1, source_target_pairs={{10,0},{12,2},{14,4},{16,6},{18,8},{20,10},{22,12},{24,14},{26,16}... | collective-permute-start | bytes 98312 | tf_op jit(solution)/shard_map/ppermute | solution.py:15
  75.6 1.3 collective-permute-done.9
  77.0 1.8 collective-permute-start.10
  78.8 1.5 collective-permute-done.10
  80.3 2.5 collective-permute-start.11
  82.8 3.7 %collective-permute-done.11 = f32[32,256]{1,0:T(8,128)S(1)} collective-permute-done((f32[32,256]{1,0:T(8,128)}, f32[32,256]{1,0:T(8,128)S(1)}, u32[]{:S(2)}, u32[]{:S(2)}) %collective-permute-start.11) | collective-permute-done | bytes 32800 | tf_op jit(solution)/shard_map/ppermute | solution.py:15
  87.2 38.6 %while.20 = (s32[]{:T(128)}, f32[32,256]{1,0:T(8,128)S(1)}, s32[]{:T(128)}, s32[8]{0:T(128)}, f32[8,32,256]{2,1,0:T(8,128)}, /*index=5*/f32[8,256,256]{2,1,0:T(8,128)}, s32[]{:T(128)}, s32[]{:T(128)}, s32[]{:T(128)}) while((s32[]{:T(128)}, f32[32,256]{1,0:T(8,128)S(1)}, s32[]{:T(128)}, s32[8]{0:T(128)}, f32[8,32,256]{2,1,0:T(8,128)}, ...), condition=%wide.region_3.6_spmd, body=%wide.region_2.5_spmd.sunk | while | flops 25174024 | bytes 360637 | solution.py:50
  125.8 3.8 %all_gather.6 = f32[64,256]{1,0:T(8,128)S(1)} all-gather(f32[32,256]{1,0:T(8,128)S(1)} %get-tuple-element.73), channel_id=1, replica_groups=mesh['leaf'=16,'sub'=2] {'sub'}, dimensions={0}, use_global_device_ids=true | all-gather | bytes 98304 | tf_op jit(solution)/shard_map/all_gather | solution.py:69
  130.3 2.5 pad_maximum_fusion
  132.7 3.6 %gather_fusion.3 = f32[8,64,512]{1,2,0:T(8,128)} fusion(f32[64,6,512]{0,2,1:T(8,128)} %bitcast.168, s32[1024]{0:T(1024)} %pad_clamp_fusion.1), kind=kCustom, calls=%fused_computation.clone | custom fusion | bytes 2097184 | tf_op jit(solution)/shard_map/jit(_take)/gather | solution.py:89
  136.3 3.2 %copy.44 = f32[8,64,512]{2,1,0:T(8,128)} copy(f32[8,64,512]{1,2,0:T(8,128)} %gather_fusion.3) | data formatting | bytes 2097152 | tf_op jit(solution)/shard_map/jit(_take)/gather | solution.py:89
  139.5 9.7 %fusion.26 = f32[64,2,512]{2,0,1:T(8,128)S(1)} fusion(f32[2,512]{1,0:T(2,128)S(1)} %copy-done.13, f32[2,4,512]{2,1,0:T(4,128)S(1)} %copy-done.5, f32[2,512]{1,0:T(2,128)S(1)} %copy-done.11, f32[2,4,512]{2,1,0:T(4,128)S(1)} %copy-done.7, f32[2,512]{1,0:T(2,128)S(1)} %copy-done.9, f32[2,4,512]{2,1,0:T(4,128)S(1)} %bitcast.184, ...), kind=kOutput, calls=%fused_computation.38 | convolution fusion | flops 1629749248 | bytes 1372168 | tf_op jit(solution)/shard_map/clnp,lnpq->clq/dot_general | solution.py:90
  150.5 39.2 %psum.7 = f32[64]{0:T(128)S(1)} all-reduce(f32[64]{0:T(128)S(1)} %get-tuple-element.109), channel_id=1, replica_groups=mesh['leaf'=16,'sub'=2] {'leaf','sub'}, use_global_device_ids=true, to_apply=%region_5.8 | all-reduce | flops 64 | bytes 512 | tf_op jit(solution)/shard_map/psum | solution.py:149
  191.7 1.5 collective-permute-start.16
  194.0 1.7 collective-permute-start.14
  199.2 10.4 %reduce-scatter.5.cloned.1.call-done = f32[32,256]{1,0:T(8,128)} async-done(((f32[64,256]{1,0:T(8,128)}), f32[32,256]{1,0:T(8,128)}) %reduce-scatter.5.cloned.1.call-update) | async-done | bytes 32784 | tf_op jit(solution)/shard_map/reduce_scatter | solution.py:66
  210.3 2.4 collective-permute-start.25
  214.0 5.3 %collective-permute-start.19 = (f32[32,256]{1,0:T(8,128)}, f32[32,256]{1,0:T(8,128)S(1)}, u32[]{:S(2)}, u32[]{:S(2)}) collective-permute-start(f32[32,256]{1,0:T(8,128)} %reduce-scatter.5.cloned.1.call-done), channel_id=1, source_target_pairs={{6,0},{8,2},{10,4},{12,6},{14,8},{16,10},{18,12},{20,14},{22,16},{... | collective-permute-start | bytes 98312 | tf_op jit(solution)/shard_map/ppermute | solution.py:15
  219.2 1.3 collective-permute-done.19
  220.6 4.5 %collective-permute-start.20 = (f32[32,256]{1,0:T(8,128)}, f32[32,256]{1,0:T(8,128)S(1)}, u32[]{:S(2)}, u32[]{:S(2)}) collective-permute-start(f32[32,256]{1,0:T(8,128)} %reduce-scatter.5.cloned.1.call-done), channel_id=1, source_target_pairs={{8,0},{10,2},{12,4},{14,6},{16,8},{18,10},{20,12},{22,14},{24,16},... | collective-permute-start | bytes 98312 | tf_op jit(solution)/shard_map/ppermute | solution.py:15
  225.0 1.3 collective-permute-done.20
  226.4 2.6 collective-permute-start.21
  229.0 1.3 collective-permute-done.21
  230.4 1.8 collective-permute-start.22
  232.2 1.3 collective-permute-done.22
  233.5 2.4 collective-permute-start.23
  235.9 4.2 %collective-permute-done.23 = f32[32,256]{1,0:T(8,128)S(1)} collective-permute-done((f32[32,256]{1,0:T(8,128)}, f32[32,256]{1,0:T(8,128)S(1)}, u32[]{:S(2)}, u32[]{:S(2)}) %collective-permute-start.23) | collective-permute-done | bytes 32800 | tf_op jit(solution)/shard_map/ppermute | solution.py:15
  240.2 42.2 %while.21 = (s32[]{:T(128)}, f32[32,256]{1,0:T(8,128)S(1)}, s32[]{:T(128)}, s32[8]{0:T(128)}, f32[8,32,256]{2,1,0:T(8,128)S(1)}, /*index=5*/f32[8,256,256]{2,1,0:T(8,128)}, s32[]{:T(128)}, s32[]{:T(128)}, s32[]{:T(128)}) while((s32[]{:T(128)}, f32[32,256]{1,0:T(8,128)S(1)}, s32[]{:T(128)}, s32[8]{0:T(128)}, f32[8,32,256]{2,1,0:T(8,128)S(1)}, ...), condition=%wide.region_8.11_spmd, body=%wide.region_7.10_spmd.sunk | while | flops 25174024 | bytes 360637 | solution.py:50
  240.8 1.3 dynamic_slice.45
  246.0 1.3 dynamic_slice.45
  251.2 1.3 dynamic_slice.45
  282.4 8.1 %all_gather.7 = f32[64,256]{1,0:T(8,128)S(1)} all-gather(f32[32,256]{1,0:T(8,128)S(1)} %get-tuple-element.74), channel_id=1, replica_groups=mesh['leaf'=16,'sub'=2] {'sub'}, dimensions={0}, use_global_device_ids=true | all-gather | bytes 98304 | tf_op jit(solution)/shard_map/all_gather | solution.py:69
  292.4 1.7 gather_fusion.5
  294.2 9.7 %fusion.27 = f32[64,2,512]{2,0,1:T(8,128)S(1)} fusion(f32[2,512]{1,0:T(2,128)S(1)} %copy-done.14, f32[2,4,512]{2,1,0:T(4,128)S(1)} %copy-done.6, f32[2,512]{1,0:T(2,128)S(1)} %copy-done.12, f32[2,4,512]{2,1,0:T(4,128)S(1)} %copy-done.8, f32[2,512]{1,0:T(2,128)S(1)} %copy-done.10, f32[2,4,512]{2,1,0:T(4,128)S(1)} %bitcast.185, ...), kind=kOutput, calls=%fused_computation.39 | convolution fusion | flops 1629749248 | bytes 1372168 | tf_op jit(solution)/shard_map/clnp,lnpq->clq/dot_general | solution.py:90
  305.2 3.3 %scatter_custom_fusion = f32[64,1024]{0,1:T(8,128)S(1)} fusion(s32[1024]{0:T(1024)} %get-tuple-element.108, f32[1024,64]{1,0:T(8,128)S(1)} %copy.49, f32[]{:T(128)} %constant.109.clone.1), kind=kCustom, calls=%fused_computation.71 | custom fusion | bytes 262656 | tf_op jit(solution)/shard_map/scatter | solution.py:163
  (166 shorter events, 73.3 us)
Async XLA Ops:
  6.5 44.5 %copy-start = (f32[4,256,256]{2,1,0:T(8,128)S(1)}, f32[4,256,256]{2,1,0:T(8,128)}, u32[]{:S(2)}) copy-start(f32[4,256,256]{2,1,0:T(8,128)} %param.26) | copy-start | bytes 3145732
  6.5 6.6 %copy-start.1 = (f32[2,512,256]{2,1,0:T(8,128)S(1)}, f32[2,512,256]{2,1,0:T(8,128)}, u32[]{:S(2)}) copy-start(f32[2,512,256]{2,1,0:T(8,128)} %param.24) | copy-start | bytes 3145732
  6.5 38.6 %reduce-scatter.3.cloned.1.call-start = ((), (), s32[]{:S(2)}) async-start(), calls=%async_computation.2 | async-start | bytes 98304 | tf_op jit(solution)/shard_map/reduce_scatter | solution.py:66
  9.1 15.4 %copy-start.2 = (f32[2,256,256]{2,1,0:T(8,128)S(1)}, f32[2,256,256]{2,1,0:T(8,128)}, u32[]{:S(2)}) copy-start(f32[2,256,256]{2,1,0:T(8,128)} %param.25) | copy-start | bytes 1572868
  13.1 13.2 %copy-start.18 = (s32[2,2]{1,0:T(2,128)S(1)}, s32[2,2]{1,0:T(2,128)}, u32[]{:S(2)}) copy-start(s32[2,2]{1,0:T(2,128)} %param.22) | copy-start | bytes 52
  13.1 16.4 %copy-start.19 = (s32[1,8]{1,0:T(1,128)S(1)}, s32[1,8]{1,0:T(1,128)}, u32[]{:S(2)}) copy-start(s32[1,8]{1,0:T(1,128)} %param.23) | copy-start | bytes 100
  13.1 17.0 %copy-start.17 = (s32[2,4]{1,0:T(2,128)S(1)}, s32[2,4]{1,0:T(2,128)}, u32[]{:S(2)}) copy-start(s32[2,4]{1,0:T(2,128)} %param.21) | copy-start | bytes 100
  15.2 28.4 %collective-permute-start.5 = (f32[2,64,256]{2,1,0:T(8,128)S(1)}, f32[2,64,256]{2,1,0:T(8,128)S(1)}, u32[]{:S(2)}, u32[]{:S(2)}) collective-permute-start(f32[2,64,256]{2,1,0:T(8,128)S(1)} %fusion.58), channel_id=1, source_target_pairs={{1,0},{2,1},{3,2},{4,3},{5,4},{6,5},{7,6},{8,7},{9,8},{10,9},{11,1... | collective-permute-start | bytes 393224 | tf_op jit(solution)/shard_map/ppermute | solution.py:15
  15.9 27.7 %collective-permute-start.4 = (f32[2,64,256]{2,1,0:T(8,128)S(1)}, f32[2,64,256]{2,1,0:T(8,128)S(1)}, u32[]{:S(2)}, u32[]{:S(2)}) collective-permute-start(f32[2,64,256]{2,1,0:T(8,128)S(1)} %fusion.58), channel_id=1, source_target_pairs={{31,0},{0,1},{1,2},{2,3},{3,4},{4,5},{5,6},{6,7},{7,8},{8,9},{9,10... | collective-permute-start | bytes 393224 | tf_op jit(solution)/shard_map/ppermute | solution.py:15
  22.7 13.9 %collective-permute-start.1 = (f32[3,1024]{0,1:T(8,128)S(1)}, f32[3,1024]{0,1:T(8,128)}, u32[]{:S(2)}, u32[]{:S(2)}) collective-permute-start(f32[3,1024]{0,1:T(8,128)S(1)} %bitcast.164), channel_id=1, source_target_pairs={{1,0},{2,1},{3,2},{4,3},{5,4},{6,5},{7,6},{8,7},{9,8},{10,9},{11,1... | collective-permute-start | bytes 36872 | tf_op jit(solution)/shard_map/ppermute | solution.py:15
  22.8 16.8 %collective-permute-start = (f32[3,1024]{0,1:T(8,128)S(1)}, f32[3,1024]{0,1:T(8,128)}, u32[]{:S(2)}, u32[]{:S(2)}) collective-permute-start(f32[3,1024]{0,1:T(8,128)S(1)} %bitcast.165), channel_id=1, source_target_pairs={{31,0},{0,1},{1,2},{2,3},{3,4},{4,5},{5,6},{6,7},{7,8},{8,9},{9,10... | collective-permute-start | bytes 36872 | tf_op jit(solution)/shard_map/ppermute | solution.py:15
  25.6 184.0 %reduce-scatter.5.cloned.1.call-start = ((), (), s32[]{:S(2)}) async-start(), calls=%async_computation.3 | async-start | bytes 98304 | tf_op jit(solution)/shard_map/reduce_scatter | solution.py:66
  25.6 104.6 %collective-permute-start.3 = (f32[64,1024]{0,1:T(8,128)}, f32[64,1024]{0,1:T(8,128)}, u32[]{:S(2)}, u32[]{:S(2)}) collective-permute-start(f32[64,1024]{0,1:T(8,128)} %bitcast.171), channel_id=1, source_target_pairs={{1,0},{2,1},{3,2},{4,3},{5,4},{6,5},{7,6},{8,7},{9,8},{10,9},{11,1... | collective-permute-start | bytes 786440 | tf_op jit(solution)/shard_map/ppermute | solution.py:15
  36.6 93.6 %collective-permute-start.2 = (f32[64,1024]{0,1:T(8,128)}, f32[64,1024]{0,1:T(8,128)}, u32[]{:S(2)}, u32[]{:S(2)}) collective-permute-start(f32[64,1024]{0,1:T(8,128)} %bitcast.172), channel_id=1, source_target_pairs={{31,0},{0,1},{1,2},{2,3},{3,4},{4,5},{5,6},{6,7},{7,8},{8,9},{9,10... | collective-permute-start | bytes 786440 | tf_op jit(solution)/shard_map/ppermute | solution.py:15
  45.1 9.7 %collective-permute-start.6 = (f32[32,256]{1,0:T(8,128)}, f32[32,256]{1,0:T(8,128)S(1)}, u32[]{:S(2)}, u32[]{:S(2)}) collective-permute-start(f32[32,256]{1,0:T(8,128)} %reduce-scatter.3.cloned.1.call-done), channel_id=1, source_target_pairs={{4,0},{6,2},{8,4},{10,6},{12,8},{14,10},{16,12},{18,14},{20,16},{2... | collective-permute-start | bytes 98312 | tf_op jit(solution)/shard_map/ppermute | solution.py:15
  51.8 78.5 %copy-start.3 = (f32[1024,64]{1,0:T(8,128)S(1)}, f32[1024,64]{1,0:T(8,128)}, u32[]{:S(2)}) copy-start(f32[1024,64]{1,0:T(8,128)} %gather_fusion.2) | copy-start | bytes 786436
  51.8 34.6 %collective-permute-start.13 = (f32[32,256]{1,0:T(8,128)}, f32[32,256]{1,0:T(8,128)S(1)}, u32[]{:S(2)}, u32[]{:S(2)}) collective-permute-start(f32[32,256]{1,0:T(8,128)} %reduce-scatter.3.cloned.1.call-done), channel_id=1, source_target_pairs={{22,0},{24,2},{26,4},{28,6},{30,8},{0,10},{2,12},{4,14},{6,16},{8,... | collective-permute-start | bytes 98312 | tf_op jit(solution)/shard_map/ppermute | solution.py:15
  53.6 32.9 %collective-permute-start.12 = (f32[32,256]{1,0:T(8,128)}, f32[32,256]{1,0:T(8,128)S(1)}, u32[]{:S(2)}, u32[]{:S(2)}) collective-permute-start(f32[32,256]{1,0:T(8,128)} %reduce-scatter.3.cloned.1.call-done), channel_id=1, source_target_pairs={{24,0},{26,2},{28,4},{30,6},{0,8},{2,10},{4,12},{6,14},{8,16},{10,... | collective-permute-start | bytes 98312 | tf_op jit(solution)/shard_map/ppermute | solution.py:15
  54.9 12.3 %collective-permute-start.7 = (f32[32,256]{1,0:T(8,128)}, f32[32,256]{1,0:T(8,128)S(1)}, u32[]{:S(2)}, u32[]{:S(2)}) collective-permute-start(f32[32,256]{1,0:T(8,128)} %reduce-scatter.3.cloned.1.call-done), channel_id=1, source_target_pairs={{6,0},{8,2},{10,4},{12,6},{14,8},{16,10},{18,12},{20,14},{22,16},{... | collective-permute-start | bytes 98312 | tf_op jit(solution)/shard_map/ppermute | solution.py:15
  67.1 3.4 %collective-permute-start.8 = (f32[32,256]{1,0:T(8,128)}, f32[32,256]{1,0:T(8,128)S(1)}, u32[]{:S(2)}, u32[]{:S(2)}) collective-permute-start(f32[32,256]{1,0:T(8,128)} %reduce-scatter.3.cloned.1.call-done), channel_id=1, source_target_pairs={{8,0},{10,2},{12,4},{14,6},{16,8},{18,10},{20,12},{22,14},{24,16},... | collective-permute-start | bytes 98312 | tf_op jit(solution)/shard_map/ppermute | solution.py:15
  70.6 6.4 %collective-permute-start.9 = (f32[32,256]{1,0:T(8,128)}, f32[32,256]{1,0:T(8,128)S(1)}, u32[]{:S(2)}, u32[]{:S(2)}) collective-permute-start(f32[32,256]{1,0:T(8,128)} %reduce-scatter.3.cloned.1.call-done), channel_id=1, source_target_pairs={{10,0},{12,2},{14,4},{16,6},{18,8},{20,10},{22,12},{24,14},{26,16}... | collective-permute-start | bytes 98312 | tf_op jit(solution)/shard_map/ppermute | solution.py:15
  77.0 3.3 %collective-permute-start.10 = (f32[32,256]{1,0:T(8,128)}, f32[32,256]{1,0:T(8,128)S(1)}, u32[]{:S(2)}, u32[]{:S(2)}) collective-permute-start(f32[32,256]{1,0:T(8,128)} %reduce-scatter.3.cloned.1.call-done), channel_id=1, source_target_pairs={{28,0},{30,2},{0,4},{2,6},{4,8},{6,10},{8,12},{10,14},{12,16},{14,... | collective-permute-start | bytes 98312 | tf_op jit(solution)/shard_map/ppermute | solution.py:15
  80.3 6.1 %collective-permute-start.11 = (f32[32,256]{1,0:T(8,128)}, f32[32,256]{1,0:T(8,128)S(1)}, u32[]{:S(2)}, u32[]{:S(2)}) collective-permute-start(f32[32,256]{1,0:T(8,128)} %reduce-scatter.3.cloned.1.call-done), channel_id=1, source_target_pairs={{26,0},{28,2},{30,4},{0,6},{2,8},{4,10},{6,12},{8,14},{10,16},{12,... | collective-permute-start | bytes 98312 | tf_op jit(solution)/shard_map/ppermute | solution.py:15
  86.5 0.7 copy-start.4
  136.3 3.2 %copy-start.5 = (f32[2,4,512]{2,1,0:T(4,128)S(1)}, f32[2,4,512]{2,1,0:T(4,128)}, u32[]{:S(2)}) copy-start(f32[2,4,512]{2,1,0:T(4,128)} %get-tuple-element.111) | copy-start | bytes 49156
  136.3 3.2 %copy-start.7 = (f32[2,4,512]{2,1,0:T(4,128)S(1)}, f32[2,4,512]{2,1,0:T(4,128)}, u32[]{:S(2)}) copy-start(f32[2,4,512]{2,1,0:T(4,128)} %get-tuple-element.112) | copy-start | bytes 49156
  136.3 3.2 %copy-start.9 = (f32[2,512]{1,0:T(2,128)S(1)}, f32[2,512]{1,0:T(2,128)}, u32[]{:S(2)}) copy-start(f32[2,512]{1,0:T(2,128)} %sub.98) | copy-start | bytes 12292
  136.3 3.2 %copy-start.11 = (f32[2,512]{1,0:T(2,128)S(1)}, f32[2,512]{1,0:T(2,128)}, u32[]{:S(2)}) copy-start(f32[2,512]{1,0:T(2,128)} %sub.103) | copy-start | bytes 12292
  136.3 3.2 %copy-start.13 = (f32[2,512]{1,0:T(2,128)S(1)}, f32[2,512]{1,0:T(2,128)}, u32[]{:S(2)}) copy-start(f32[2,512]{1,0:T(2,128)} %sub.108) | copy-start | bytes 12292
  136.3 3.2 %copy-start.15 = (pred[2,4]{1,0:T(4,128)(4,1)S(1)}, pred[2,4]{1,0:T(4,128)(4,1)}, u32[]{:S(2)}) copy-start(pred[2,4]{1,0:T(4,128)(4,1)} %get-tuple-element.102) | copy-start | bytes 28
  190.5 6.3 %collective-permute-start.17 = (f32[2,64,256]{2,1,0:T(8,128)S(1)}, f32[2,64,256]{2,1,0:T(8,128)S(1)}, u32[]{:S(2)}, u32[]{:S(2)}) collective-permute-start(f32[2,64,256]{2,1,0:T(8,128)S(1)} %fusion.41), channel_id=1, source_target_pairs={{1,0},{2,1},{3,2},{4,3},{5,4},{6,5},{7,6},{8,7},{9,8},{10,9},{11,1... | collective-permute-start | bytes 393224 | tf_op jit(solution)/shard_map/ppermute | solution.py:15
  191.7 5.1 %collective-permute-start.16 = (f32[2,64,256]{2,1,0:T(8,128)S(1)}, f32[2,64,256]{2,1,0:T(8,128)}, u32[]{:S(2)}, u32[]{:S(2)}) collective-permute-start(f32[2,64,256]{2,1,0:T(8,128)S(1)} %fusion.41), channel_id=1, source_target_pairs={{31,0},{0,1},{1,2},{2,3},{3,4},{4,5},{5,6},{6,7},{7,8},{8,9},{9,10... | collective-permute-start | bytes 393224 | tf_op jit(solution)/shard_map/ppermute | solution.py:15
  194.0 97.1 %collective-permute-start.15 = (f32[64,1024]{1,0:T(8,128)}, f32[64,1024]{1,0:T(8,128)}, u32[]{:S(2)}, u32[]{:S(2)}) collective-permute-start(f32[64,1024]{1,0:T(8,128)} %broadcast_multiply_fusion), channel_id=1, source_target_pairs={{1,0},{2,1},{3,2},{4,3},{5,4},{6,5},{7,6},{8,7},{9,8},{10,9},{11,1... | collective-permute-start | bytes 786440 | tf_op jit(solution)/shard_map/ppermute | solution.py:15
  194.0 97.1 %collective-permute-start.14 = (f32[64,1024]{1,0:T(8,128)}, f32[64,1024]{1,0:T(8,128)}, u32[]{:S(2)}, u32[]{:S(2)}) collective-permute-start(f32[64,1024]{1,0:T(8,128)} %broadcast_multiply_fusion), channel_id=1, source_target_pairs={{31,0},{0,1},{1,2},{2,3},{3,4},{4,5},{5,6},{6,7},{7,8},{8,9},{9,10... | collective-permute-start | bytes 786440 | tf_op jit(solution)/shard_map/ppermute | solution.py:15
  209.6 4.4 %collective-permute-start.18 = (f32[32,256]{1,0:T(8,128)}, f32[32,256]{1,0:T(8,128)S(1)}, u32[]{:S(2)}, u32[]{:S(2)}) collective-permute-start(f32[32,256]{1,0:T(8,128)} %reduce-scatter.5.cloned.1.call-done), channel_id=1, source_target_pairs={{4,0},{6,2},{8,4},{10,6},{12,8},{14,10},{16,12},{18,14},{20,16},{2... | collective-permute-start | bytes 98312 | tf_op jit(solution)/shard_map/ppermute | solution.py:15
  210.3 29.8 %collective-permute-start.25 = (f32[32,256]{1,0:T(8,128)}, f32[32,256]{1,0:T(8,128)S(1)}, u32[]{:S(2)}, u32[]{:S(2)}) collective-permute-start(f32[32,256]{1,0:T(8,128)} %reduce-scatter.5.cloned.1.call-done), channel_id=1, source_target_pairs={{22,0},{24,2},{26,4},{28,6},{30,8},{0,10},{2,12},{4,14},{6,16},{8,... | collective-permute-start | bytes 98312 | tf_op jit(solution)/shard_map/ppermute | solution.py:15
  212.8 27.4 %collective-permute-start.24 = (f32[32,256]{1,0:T(8,128)}, f32[32,256]{1,0:T(8,128)S(1)}, u32[]{:S(2)}, u32[]{:S(2)}) collective-permute-start(f32[32,256]{1,0:T(8,128)} %reduce-scatter.5.cloned.1.call-done), channel_id=1, source_target_pairs={{24,0},{26,2},{28,4},{30,6},{0,8},{2,10},{4,12},{6,14},{8,16},{10,... | collective-permute-start | bytes 98312 | tf_op jit(solution)/shard_map/ppermute | solution.py:15
  214.0 6.6 %collective-permute-start.19 = (f32[32,256]{1,0:T(8,128)}, f32[32,256]{1,0:T(8,128)S(1)}, u32[]{:S(2)}, u32[]{:S(2)}) collective-permute-start(f32[32,256]{1,0:T(8,128)} %reduce-scatter.5.cloned.1.call-done), channel_id=1, source_target_pairs={{6,0},{8,2},{10,4},{12,6},{14,8},{16,10},{18,12},{20,14},{22,16},{... | collective-permute-start | bytes 98312 | tf_op jit(solution)/shard_map/ppermute | solution.py:15
  220.6 5.8 %collective-permute-start.20 = (f32[32,256]{1,0:T(8,128)}, f32[32,256]{1,0:T(8,128)S(1)}, u32[]{:S(2)}, u32[]{:S(2)}) collective-permute-start(f32[32,256]{1,0:T(8,128)} %reduce-scatter.5.cloned.1.call-done), channel_id=1, source_target_pairs={{8,0},{10,2},{12,4},{14,6},{16,8},{18,10},{20,12},{22,14},{24,16},... | collective-permute-start | bytes 98312 | tf_op jit(solution)/shard_map/ppermute | solution.py:15
  226.4 4.0 %collective-permute-start.21 = (f32[32,256]{1,0:T(8,128)}, f32[32,256]{1,0:T(8,128)S(1)}, u32[]{:S(2)}, u32[]{:S(2)}) collective-permute-start(f32[32,256]{1,0:T(8,128)} %reduce-scatter.5.cloned.1.call-done), channel_id=1, source_target_pairs={{10,0},{12,2},{14,4},{16,6},{18,8},{20,10},{22,12},{24,14},{26,16}... | collective-permute-start | bytes 98312 | tf_op jit(solution)/shard_map/ppermute | solution.py:15
  230.4 3.2 %collective-permute-start.22 = (f32[32,256]{1,0:T(8,128)}, f32[32,256]{1,0:T(8,128)S(1)}, u32[]{:S(2)}, u32[]{:S(2)}) collective-permute-start(f32[32,256]{1,0:T(8,128)} %reduce-scatter.5.cloned.1.call-done), channel_id=1, source_target_pairs={{28,0},{30,2},{0,4},{2,6},{4,8},{6,10},{8,12},{10,14},{12,16},{14,... | collective-permute-start | bytes 98312 | tf_op jit(solution)/shard_map/ppermute | solution.py:15
  233.5 6.6 %collective-permute-start.23 = (f32[32,256]{1,0:T(8,128)}, f32[32,256]{1,0:T(8,128)S(1)}, u32[]{:S(2)}, u32[]{:S(2)}) collective-permute-start(f32[32,256]{1,0:T(8,128)} %reduce-scatter.5.cloned.1.call-done), channel_id=1, source_target_pairs={{26,0},{28,2},{30,4},{0,6},{2,8},{4,10},{6,12},{8,14},{10,16},{12,... | collective-permute-start | bytes 98312 | tf_op jit(solution)/shard_map/ppermute | solution.py:15
  292.3 1.8 copy-start.6
  292.3 1.8 copy-start.8
  292.3 1.8 copy-start.10
  292.3 1.8 copy-start.12
  292.3 1.8 copy-start.14
  292.3 1.8 copy-start.16
  (1 other events, 0.6 us)
Sparse Core Ops, SparseCore 0:
  25.7 16.0 reduce-scatter.2
  196.9 12.6 reduce-scatter.4
where the time goes:
time: 318 us; the launch traced here: 316 us
  starting transfers between devices  59.5 us (19%)
  local copies, waits for them, and re-layouts  57 us (18%)
  blocking collectives  51.2 us (16%)
  matrix products  48.7 us (15%)
  loops' own time  41 us (13%)
  waiting for transfers between devices  31.1 us (10%)
  other arithmetic  13.9 us (4%)
  between operations  13.9 us (4%)
    ppermute x26, starting transfers between devices, from_behind(): return lax.ppermute(block, axis, route)  59.5 us
    another operation x2, loops' own time, couple_chips(): return lax.fori_loop(0, used_count, add_slot, start_value)  41 us
    psum x1, blocking collectives, on_device(): lax.psum(jnp.sum(first_pass * first_pass, axis=1), ('leaf', 'sub'))  39.2 us
    ppermute x26, waiting for transfers between devices, from_behind(): return lax.ppermute(block, axis, route)  20.7 us
    dynamic_slice x16, local copies, waits for them, and re-layouts, add_slot(): source = stacked[slot_place[slot_index]]  20.5 us
    dot_general x2, matrix products, apply_matrix(): jnp.einsum('clnp,lnpq->clq', source_values, kernels, precision=highest)  19.5 us
    dot_general x16, matrix products, add_slot(): jnp.dot(source, far_chip_blocks[slot_index], precision=highest, preferred...  19.2 us
    all_gather x2, blocking collectives, chip_level(): coupled = lax.all_gather(coupled_half, 'sub', axis=0, tiled=True)  11.9 us
  transfers between devices with their start and end apart: 28, of which 11 were waited for; matrix products, arithmetic and copies ran while one was open for 22% of the time, Pallas kernels for 0%

commit v1 on v0

--- a/solution.py
+++ b/solution.py
@@ -146,7 +146,8 @@
         far_chip_blocks,
         leaf_total,
     )
-    squares = lax.psum(jnp.sum(first_pass * first_pass, axis=1), ("leaf", "sub"))
+    one_axis = lax.psum(jnp.sum(first_pass * first_pass, axis=1), "leaf")
+    squares = lax.psum(one_axis, "sub")
     column_scale = lax.rsqrt(squares / point_total + epsilon)
     second = apply_matrix(
         first_pass * column_scale[:, None],

time: 318 us -> 318 us (level)
  blocking collectives: 51.2 us -> 46.2 us
  loops' own time: 41 us -> 44.2 us
    psum x1 -> x2, blocking collectives: 39.2 us -> 34.3 us  [the longest x1 24.8 us: on_device(): one_axis = lax.psum(jnp.sum(first_pass * first_pass, axis=1), 'leaf')]
where the time goes in v1:
time: 318 us; the launch traced here: 316 us
  starting transfers between devices  60.9 us (19%)
  local copies, waits for them, and re-layouts  56.2 us (18%)
  matrix products  48.7 us (15%)
  blocking collectives  46.2 us (15%)
  loops' own time  44.2 us (14%)
  waiting for transfers between devices  32.6 us (10%)
  between operations  13.9 us (4%)
  other arithmetic  13.7 us (4%)
    ppermute x26, starting transfers between devices, from_behind(): return lax.ppermute(block, axis, route)  60.9 us
    another operation x2, loops' own time, couple_chips(): return lax.fori_loop(0, used_count, add_slot, start_value)  44.2 us
    psum x1, blocking collectives, on_device(): one_axis = lax.psum(jnp.sum(first_pass * first_pass, axis=1), 'leaf')  24.8 us
    ppermute x26, waiting for transfers between devices, from_behind(): return lax.ppermute(block, axis, route)  20.7 us
    dynamic_slice x16, local copies, waits for them, and re-layouts, add_slot(): source = stacked[slot_place[slot_index]]  19.7 us
    dot_general x2, matrix products, apply_matrix(): jnp.einsum('clnp,lnpq->clq', source_values, kernels, precision=highest)  19.5 us
    dot_general x16, matrix products, add_slot(): jnp.dot(source, far_chip_blocks[slot_index], precision=highest, preferred...  19.2 us
    reduce_scatter x2, waiting for transfers between devices, chip_level(): halves = lax.psum_scatter(upward, 'sub', scatter_dimension=0, tiled=True)  12 us
  transfers between devices with their start and end apart: 28, of which 11 were waited for; matrix products, arithmetic and copies ran while one was open for 22% of the time, Pallas kernels for 0%

profile of v1, /device:TPU:5, one launch (start us, length us, event | category | flops | bytes accessed | tf_op | source)
XLA Modules:
  0.0 316.5 jit_solution(16943863681269111349)
XLA Ops:
  6.5 1.4 broadcast_clamp_fusion
  9.1 4.0 %gather_fusion.2 = f32[1024,64]{1,0:T(8,128)} fusion(f32[64,1024]{0,1:T(8,128)S(1)} %copy.43, s32[1024]{0:T(1024)S(1)} %get-tuple-element.107), kind=kCustom, calls=%fused_computation.6 | custom fusion | bytes 528384 | tf_op jit(solution)/shard_map/gather | solution.py:129
  13.2 2.1 fusion.58
  17.2 1.8 copy.39
  18.9 3.8 %gather_fusion = f32[1024,3]{1,0:T(8,128)S(1)} fusion(f32[3,1024]{0,1:T(8,128)} %copy.39, s32[1024]{0:T(1024)S(1)} %get-tuple-element.107), kind=kCustom, calls=%fused_computation.4 | custom fusion | bytes 28672 | tf_op jit(solution)/shard_map/gather | solution.py:130
  22.8 1.7 collective-permute-start
  28.1 1.4 slice_reduce_fusion.2
  32.8 1.3 sub.98
  37.7 1.8 copy.42
  45.1 5.9 %collective-permute-start.6 = (f32[32,256]{1,0:T(8,128)}, f32[32,256]{1,0:T(8,128)S(1)}, u32[]{:S(2)}, u32[]{:S(2)}) collective-permute-start(f32[32,256]{1,0:T(8,128)} %reduce-scatter.3.cloned.1.call-done), channel_id=1, source_target_pairs={{4,0},{6,2},{8,4},{10,6},{12,8},{14,10},{16,12},{18,14},{20,16},{2... | collective-permute-start | bytes 98312 | tf_op jit(solution)/shard_map/ppermute | solution.py:15
  51.8 1.8 collective-permute-start.13
  53.5 1.3 collective-permute-start.12
  54.8 10.9 %collective-permute-start.7 = (f32[32,256]{1,0:T(8,128)}, f32[32,256]{1,0:T(8,128)S(1)}, u32[]{:S(2)}, u32[]{:S(2)}) collective-permute-start(f32[32,256]{1,0:T(8,128)} %reduce-scatter.3.cloned.1.call-done), channel_id=1, source_target_pairs={{6,0},{8,2},{10,4},{12,6},{14,8},{16,10},{18,12},{20,14},{22,16},{... | collective-permute-start | bytes 98312 | tf_op jit(solution)/shard_map/ppermute | solution.py:15
  65.8 1.3 collective-permute-done.7
  67.3 3.2 %collective-permute-done.8 = f32[32,256]{1,0:T(8,128)S(1)} collective-permute-done((f32[32,256]{1,0:T(8,128)}, f32[32,256]{1,0:T(8,128)S(1)}, u32[]{:S(2)}, u32[]{:S(2)}) %collective-permute-start.8) | collective-permute-done | bytes 32800 | tf_op jit(solution)/shard_map/ppermute | solution.py:15
  70.5 5.1 %collective-permute-start.9 = (f32[32,256]{1,0:T(8,128)}, f32[32,256]{1,0:T(8,128)S(1)}, u32[]{:S(2)}, u32[]{:S(2)}) collective-permute-start(f32[32,256]{1,0:T(8,128)} %reduce-scatter.3.cloned.1.call-done), channel_id=1, source_target_pairs={{10,0},{12,2},{14,4},{16,6},{18,8},{20,10},{22,12},{24,14},{26,16}... | collective-permute-start | bytes 98312 | tf_op jit(solution)/shard_map/ppermute | solution.py:15
  75.6 1.3 collective-permute-done.9
  77.0 1.8 collective-permute-start.10
  78.8 1.5 collective-permute-done.10
  80.3 2.5 collective-permute-start.11
  82.7 3.7 %collective-permute-done.11 = f32[32,256]{1,0:T(8,128)S(1)} collective-permute-done((f32[32,256]{1,0:T(8,128)}, f32[32,256]{1,0:T(8,128)S(1)}, u32[]{:S(2)}, u32[]{:S(2)}) %collective-permute-start.11) | collective-permute-done | bytes 32800 | tf_op jit(solution)/shard_map/ppermute | solution.py:15
  87.1 41.1 %while.20 = (s32[]{:T(128)}, f32[32,256]{1,0:T(8,128)S(1)}, s32[]{:T(128)}, s32[8]{0:T(128)}, f32[8,32,256]{2,1,0:T(8,128)}, /*index=5*/f32[8,256,256]{2,1,0:T(8,128)}, s32[]{:T(128)}, s32[]{:T(128)}, s32[]{:T(128)}) while((s32[]{:T(128)}, f32[32,256]{1,0:T(8,128)S(1)}, s32[]{:T(128)}, s32[8]{0:T(128)}, f32[8,32,256]{2,1,0:T(8,128)}, ...), condition=%wide.region_3.6_spmd, body=%wide.region_2.5_spmd.sunk | while | flops 25174024 | bytes 360637 | solution.py:50
  128.3 3.8 %all_gather.6 = f32[64,256]{1,0:T(8,128)S(1)} all-gather(f32[32,256]{1,0:T(8,128)S(1)} %get-tuple-element.73), channel_id=1, replica_groups=mesh['leaf'=16,'sub'=2] {'sub'}, dimensions={0}, use_global_device_ids=true | all-gather | bytes 98304 | tf_op jit(solution)/shard_map/all_gather | solution.py:69
  132.7 2.4 pad_maximum_fusion
  135.2 3.6 %gather_fusion.3 = f32[8,64,512]{1,2,0:T(8,128)} fusion(f32[64,6,512]{0,2,1:T(8,128)} %bitcast.168, s32[1024]{0:T(1024)} %pad_clamp_fusion.1), kind=kCustom, calls=%fused_computation.clone | custom fusion | bytes 2097184 | tf_op jit(solution)/shard_map/jit(_take)/gather | solution.py:89
  138.8 3.2 %copy.44 = f32[8,64,512]{2,1,0:T(8,128)} copy(f32[8,64,512]{1,2,0:T(8,128)} %gather_fusion.3) | data formatting | bytes 2097152 | tf_op jit(solution)/shard_map/jit(_take)/gather | solution.py:89
  142.0 9.7 %fusion.26 = f32[64,2,512]{2,0,1:T(8,128)S(1)} fusion(f32[2,512]{1,0:T(2,128)S(1)} %copy-done.13, f32[2,4,512]{2,1,0:T(4,128)S(1)} %copy-done.5, f32[2,512]{1,0:T(2,128)S(1)} %copy-done.11, f32[2,4,512]{2,1,0:T(4,128)S(1)} %copy-done.7, f32[2,512]{1,0:T(2,128)S(1)} %copy-done.9, f32[2,4,512]{2,1,0:T(4,128)S(1)} %bitcast.184, ...), kind=kOutput, calls=%fused_computation.38 | convolution fusion | flops 1629749248 | bytes 1372168 | tf_op jit(solution)/shard_map/clnp,lnpq->clq/dot_general | solution.py:90
  153.0 24.8 %psum.14 = f32[64]{0:T(128)S(1)} all-reduce(f32[64]{0:T(128)S(1)} %get-tuple-element.109), channel_id=1, replica_groups=mesh['leaf'=16,'sub'=2] {'leaf'}, use_global_device_ids=true, to_apply=%region_5.8 | all-reduce | flops 64 | bytes 512 | tf_op jit(solution)/shard_map/psum | solution.py:149
  177.8 9.5 %psum.15 = f32[64]{0:T(128)S(1)} all-reduce(f32[64]{0:T(128)S(1)} %psum.14), channel_id=1, replica_groups=mesh['leaf'=16,'sub'=2] {'sub'}, use_global_device_ids=true, to_apply=%region_6.9 | all-reduce | flops 64 | bytes 512 | tf_op jit(solution)/shard_map/psum | solution.py:150
  188.4 1.7 collective-permute-start.16
  190.9 3.7 %collective-permute-start.15 = (f32[64,1024]{1,0:T(8,128)}, f32[64,1024]{1,0:T(8,128)}, u32[]{:S(2)}, u32[]{:S(2)}) collective-permute-start(f32[64,1024]{1,0:T(8,128)} %broadcast_multiply_fusion), channel_id=1, source_target_pairs={{1,0},{2,1},{3,2},{4,3},{5,4},{6,5},{7,6},{8,7},{9,8},{10,9},{11,1... | collective-permute-start | bytes 786440 | tf_op jit(solution)/shard_map/ppermute | solution.py:15
  198.0 11.9 %reduce-scatter.5.cloned.1.call-done = f32[32,256]{1,0:T(8,128)} async-done(((f32[64,256]{1,0:T(8,128)}), f32[32,256]{1,0:T(8,128)}) %reduce-scatter.5.cloned.1.call-update) | async-done | bytes 32784 | tf_op jit(solution)/shard_map/reduce_scatter | solution.py:66
  210.7 2.4 collective-permute-start.25
  214.3 5.3 %collective-permute-start.19 = (f32[32,256]{1,0:T(8,128)}, f32[32,256]{1,0:T(8,128)S(1)}, u32[]{:S(2)}, u32[]{:S(2)}) collective-permute-start(f32[32,256]{1,0:T(8,128)} %reduce-scatter.5.cloned.1.call-done), channel_id=1, source_target_pairs={{6,0},{8,2},{10,4},{12,6},{14,8},{16,10},{18,12},{20,14},{22,16},{... | collective-permute-start | bytes 98312 | tf_op jit(solution)/shard_map/ppermute | solution.py:15
  219.6 1.3 collective-permute-done.19
  220.9 4.5 %collective-permute-start.20 = (f32[32,256]{1,0:T(8,128)}, f32[32,256]{1,0:T(8,128)S(1)}, u32[]{:S(2)}, u32[]{:S(2)}) collective-permute-start(f32[32,256]{1,0:T(8,128)} %reduce-scatter.5.cloned.1.call-done), channel_id=1, source_target_pairs={{8,0},{10,2},{12,4},{14,6},{16,8},{18,10},{20,12},{22,14},{24,16},... | collective-permute-start | bytes 98312 | tf_op jit(solution)/shard_map/ppermute | solution.py:15
  225.4 1.3 collective-permute-done.20
  226.7 2.7 collective-permute-start.21
  229.4 1.3 collective-permute-done.21
  230.7 1.8 collective-permute-start.22
  232.5 1.3 collective-permute-done.22
  233.9 2.4 collective-permute-start.23
  236.2 4.2 %collective-permute-done.23 = f32[32,256]{1,0:T(8,128)S(1)} collective-permute-done((f32[32,256]{1,0:T(8,128)}, f32[32,256]{1,0:T(8,128)S(1)}, u32[]{:S(2)}, u32[]{:S(2)}) %collective-permute-start.23) | collective-permute-done | bytes 32800 | tf_op jit(solution)/shard_map/ppermute | solution.py:15
  240.5 42.0 %while.21 = (s32[]{:T(128)}, f32[32,256]{1,0:T(8,128)S(1)}, s32[]{:T(128)}, s32[8]{0:T(128)}, f32[8,32,256]{2,1,0:T(8,128)S(1)}, /*index=5*/f32[8,256,256]{2,1,0:T(8,128)}, s32[]{:T(128)}, s32[]{:T(128)}, s32[]{:T(128)}) while((s32[]{:T(128)}, f32[32,256]{1,0:T(8,128)S(1)}, s32[]{:T(128)}, s32[8]{0:T(128)}, f32[8,32,256]{2,1,0:T(8,128)S(1)}, ...), condition=%wide.region_9.12_spmd, body=%wide.region_8.11_spmd.sunk | while | flops 25174024 | bytes 360637 | solution.py:50
  282.5 8.1 %all_gather.7 = f32[64,256]{1,0:T(8,128)S(1)} all-gather(f32[32,256]{1,0:T(8,128)S(1)} %get-tuple-element.74), channel_id=1, replica_groups=mesh['leaf'=16,'sub'=2] {'sub'}, dimensions={0}, use_global_device_ids=true | all-gather | bytes 98304 | tf_op jit(solution)/shard_map/all_gather | solution.py:69
  292.5 1.7 gather_fusion.5
  294.3 9.7 %fusion.27 = f32[64,2,512]{2,0,1:T(8,128)S(1)} fusion(f32[2,512]{1,0:T(2,128)S(1)} %copy-done.14, f32[2,4,512]{2,1,0:T(4,128)S(1)} %copy-done.6, f32[2,512]{1,0:T(2,128)S(1)} %copy-done.12, f32[2,4,512]{2,1,0:T(4,128)S(1)} %copy-done.8, f32[2,512]{1,0:T(2,128)S(1)} %copy-done.10, f32[2,4,512]{2,1,0:T(4,128)S(1)} %bitcast.185, ...), kind=kOutput, calls=%fused_computation.39 | convolution fusion | flops 1629749248 | bytes 1372168 | tf_op jit(solution)/shard_map/clnp,lnpq->clq/dot_general | solution.py:90
  305.4 3.3 %scatter_custom_fusion = f32[64,1024]{0,1:T(8,128)S(1)} fusion(s32[1024]{0:T(1024)} %get-tuple-element.108, f32[1024,64]{1,0:T(8,128)S(1)} %copy.49, f32[]{:T(128)} %constant.109.clone.1), kind=kCustom, calls=%fused_computation.71 | custom fusion | bytes 262656 | tf_op jit(solution)/shard_map/scatter | solution.py:164
  (167 shorter events, 73.0 us)
Async XLA Ops:
  6.5 44.5 %copy-start = (f32[4,256,256]{2,1,0:T(8,128)S(1)}, f32[4,256,256]{2,1,0:T(8,128)}, u32[]{:S(2)}) copy-start(f32[4,256,256]{2,1,0:T(8,128)} %param.26) | copy-start | bytes 3145732
  6.5 6.6 %copy-start.1 = (f32[2,512,256]{2,1,0:T(8,128)S(1)}, f32[2,512,256]{2,1,0:T(8,128)}, u32[]{:S(2)}) copy-start(f32[2,512,256]{2,1,0:T(8,128)} %param.24) | copy-start | bytes 3145732
  6.5 38.6 %reduce-scatter.3.cloned.1.call-start = ((), (), s32[]{:S(2)}) async-start(), calls=%async_computation.2 | async-start | bytes 98304 | tf_op jit(solution)/shard_map/reduce_scatter | solution.py:66
  9.1 15.5 %copy-start.2 = (f32[2,256,256]{2,1,0:T(8,128)S(1)}, f32[2,256,256]{2,1,0:T(8,128)}, u32[]{:S(2)}) copy-start(f32[2,256,256]{2,1,0:T(8,128)} %param.25) | copy-start | bytes 1572868
  13.2 13.2 %copy-start.18 = (s32[2,2]{1,0:T(2,128)S(1)}, s32[2,2]{1,0:T(2,128)}, u32[]{:S(2)}) copy-start(s32[2,2]{1,0:T(2,128)} %param.22) | copy-start | bytes 52
  13.2 16.3 %copy-start.19 = (s32[1,8]{1,0:T(1,128)S(1)}, s32[1,8]{1,0:T(1,128)}, u32[]{:S(2)}) copy-start(s32[1,8]{1,0:T(1,128)} %param.23) | copy-start | bytes 100
  13.2 16.8 %copy-start.17 = (s32[2,4]{1,0:T(2,128)S(1)}, s32[2,4]{1,0:T(2,128)}, u32[]{:S(2)}) copy-start(s32[2,4]{1,0:T(2,128)} %param.21) | copy-start | bytes 100
  15.3 28.4 %collective-permute-start.5 = (f32[2,64,256]{2,1,0:T(8,128)S(1)}, f32[2,64,256]{2,1,0:T(8,128)S(1)}, u32[]{:S(2)}, u32[]{:S(2)}) collective-permute-start(f32[2,64,256]{2,1,0:T(8,128)S(1)} %fusion.58), channel_id=1, source_target_pairs={{1,0},{2,1},{3,2},{4,3},{5,4},{6,5},{7,6},{8,7},{9,8},{10,9},{11,1... | collective-permute-start | bytes 393224 | tf_op jit(solution)/shard_map/ppermute | solution.py:15
  16.0 27.7 %collective-permute-start.4 = (f32[2,64,256]{2,1,0:T(8,128)S(1)}, f32[2,64,256]{2,1,0:T(8,128)S(1)}, u32[]{:S(2)}, u32[]{:S(2)}) collective-permute-start(f32[2,64,256]{2,1,0:T(8,128)S(1)} %fusion.58), channel_id=1, source_target_pairs={{31,0},{0,1},{1,2},{2,3},{3,4},{4,5},{5,6},{6,7},{7,8},{8,9},{9,10... | collective-permute-start | bytes 393224 | tf_op jit(solution)/shard_map/ppermute | solution.py:15
  22.8 13.8 %collective-permute-start.1 = (f32[3,1024]{0,1:T(8,128)S(1)}, f32[3,1024]{0,1:T(8,128)}, u32[]{:S(2)}, u32[]{:S(2)}) collective-permute-start(f32[3,1024]{0,1:T(8,128)S(1)} %bitcast.164), channel_id=1, source_target_pairs={{1,0},{2,1},{3,2},{4,3},{5,4},{6,5},{7,6},{8,7},{9,8},{10,9},{11,1... | collective-permute-start | bytes 36872 | tf_op jit(solution)/shard_map/ppermute | solution.py:15
  22.8 16.7 %collective-permute-start = (f32[3,1024]{0,1:T(8,128)S(1)}, f32[3,1024]{0,1:T(8,128)}, u32[]{:S(2)}, u32[]{:S(2)}) collective-permute-start(f32[3,1024]{0,1:T(8,128)S(1)} %bitcast.165), channel_id=1, source_target_pairs={{31,0},{0,1},{1,2},{2,3},{3,4},{4,5},{5,6},{6,7},{7,8},{8,9},{9,10... | collective-permute-start | bytes 36872 | tf_op jit(solution)/shard_map/ppermute | solution.py:15
  25.6 184.3 %reduce-scatter.5.cloned.1.call-start = ((), (), s32[]{:S(2)}) async-start(), calls=%async_computation.3 | async-start | bytes 98304 | tf_op jit(solution)/shard_map/reduce_scatter | solution.py:66
  25.7 107.0 %collective-permute-start.3 = (f32[64,1024]{0,1:T(8,128)}, f32[64,1024]{0,1:T(8,128)}, u32[]{:S(2)}, u32[]{:S(2)}) collective-permute-start(f32[64,1024]{0,1:T(8,128)} %bitcast.171), channel_id=1, source_target_pairs={{1,0},{2,1},{3,2},{4,3},{5,4},{6,5},{7,6},{8,7},{9,8},{10,9},{11,1... | collective-permute-start | bytes 786440 | tf_op jit(solution)/shard_map/ppermute | solution.py:15
  36.6 96.1 %collective-permute-start.2 = (f32[64,1024]{0,1:T(8,128)}, f32[64,1024]{0,1:T(8,128)}, u32[]{:S(2)}, u32[]{:S(2)}) collective-permute-start(f32[64,1024]{0,1:T(8,128)} %bitcast.172), channel_id=1, source_target_pairs={{31,0},{0,1},{1,2},{2,3},{3,4},{4,5},{5,6},{6,7},{7,8},{8,9},{9,10... | collective-permute-start | bytes 786440 | tf_op jit(solution)/shard_map/ppermute | solution.py:15
  45.1 9.7 %collective-permute-start.6 = (f32[32,256]{1,0:T(8,128)}, f32[32,256]{1,0:T(8,128)S(1)}, u32[]{:S(2)}, u32[]{:S(2)}) collective-permute-start(f32[32,256]{1,0:T(8,128)} %reduce-scatter.3.cloned.1.call-done), channel_id=1, source_target_pairs={{4,0},{6,2},{8,4},{10,6},{12,8},{14,10},{16,12},{18,14},{20,16},{2... | collective-permute-start | bytes 98312 | tf_op jit(solution)/shard_map/ppermute | solution.py:15
  51.8 80.9 %copy-start.3 = (f32[1024,64]{1,0:T(8,128)S(1)}, f32[1024,64]{1,0:T(8,128)}, u32[]{:S(2)}) copy-start(f32[1024,64]{1,0:T(8,128)} %gather_fusion.2) | copy-start | bytes 786436
  51.8 34.6 %collective-permute-start.13 = (f32[32,256]{1,0:T(8,128)}, f32[32,256]{1,0:T(8,128)S(1)}, u32[]{:S(2)}, u32[]{:S(2)}) collective-permute-start(f32[32,256]{1,0:T(8,128)} %reduce-scatter.3.cloned.1.call-done), channel_id=1, source_target_pairs={{22,0},{24,2},{26,4},{28,6},{30,8},{0,10},{2,12},{4,14},{6,16},{8,... | collective-permute-start | bytes 98312 | tf_op jit(solution)/shard_map/ppermute | solution.py:15
  53.5 32.9 %collective-permute-start.12 = (f32[32,256]{1,0:T(8,128)}, f32[32,256]{1,0:T(8,128)S(1)}, u32[]{:S(2)}, u32[]{:S(2)}) collective-permute-start(f32[32,256]{1,0:T(8,128)} %reduce-scatter.3.cloned.1.call-done), channel_id=1, source_target_pairs={{24,0},{26,2},{28,4},{30,6},{0,8},{2,10},{4,12},{6,14},{8,16},{10,... | collective-permute-start | bytes 98312 | tf_op jit(solution)/shard_map/ppermute | solution.py:15
  54.8 12.3 %collective-permute-start.7 = (f32[32,256]{1,0:T(8,128)}, f32[32,256]{1,0:T(8,128)S(1)}, u32[]{:S(2)}, u32[]{:S(2)}) collective-permute-start(f32[32,256]{1,0:T(8,128)} %reduce-scatter.3.cloned.1.call-done), channel_id=1, source_target_pairs={{6,0},{8,2},{10,4},{12,6},{14,8},{16,10},{18,12},{20,14},{22,16},{... | collective-permute-start | bytes 98312 | tf_op jit(solution)/shard_map/ppermute | solution.py:15
  67.1 3.4 %collective-permute-start.8 = (f32[32,256]{1,0:T(8,128)}, f32[32,256]{1,0:T(8,128)S(1)}, u32[]{:S(2)}, u32[]{:S(2)}) collective-permute-start(f32[32,256]{1,0:T(8,128)} %reduce-scatter.3.cloned.1.call-done), channel_id=1, source_target_pairs={{8,0},{10,2},{12,4},{14,6},{16,8},{18,10},{20,12},{22,14},{24,16},... | collective-permute-start | bytes 98312 | tf_op jit(solution)/shard_map/ppermute | solution.py:15
  70.5 6.4 %collective-permute-start.9 = (f32[32,256]{1,0:T(8,128)}, f32[32,256]{1,0:T(8,128)S(1)}, u32[]{:S(2)}, u32[]{:S(2)}) collective-permute-start(f32[32,256]{1,0:T(8,128)} %reduce-scatter.3.cloned.1.call-done), channel_id=1, source_target_pairs={{10,0},{12,2},{14,4},{16,6},{18,8},{20,10},{22,12},{24,14},{26,16}... | collective-permute-start | bytes 98312 | tf_op jit(solution)/shard_map/ppermute | solution.py:15
  77.0 3.3 %collective-permute-start.10 = (f32[32,256]{1,0:T(8,128)}, f32[32,256]{1,0:T(8,128)S(1)}, u32[]{:S(2)}, u32[]{:S(2)}) collective-permute-start(f32[32,256]{1,0:T(8,128)} %reduce-scatter.3.cloned.1.call-done), channel_id=1, source_target_pairs={{28,0},{30,2},{0,4},{2,6},{4,8},{6,10},{8,12},{10,14},{12,16},{14,... | collective-permute-start | bytes 98312 | tf_op jit(solution)/shard_map/ppermute | solution.py:15
  80.3 6.1 %collective-permute-start.11 = (f32[32,256]{1,0:T(8,128)}, f32[32,256]{1,0:T(8,128)S(1)}, u32[]{:S(2)}, u32[]{:S(2)}) collective-permute-start(f32[32,256]{1,0:T(8,128)} %reduce-scatter.3.cloned.1.call-done), channel_id=1, source_target_pairs={{26,0},{28,2},{30,4},{0,6},{2,8},{4,10},{6,12},{8,14},{10,16},{12,... | collective-permute-start | bytes 98312 | tf_op jit(solution)/shard_map/ppermute | solution.py:15
  86.4 0.7 copy-start.4
  138.7 3.2 %copy-start.5 = (f32[2,4,512]{2,1,0:T(4,128)S(1)}, f32[2,4,512]{2,1,0:T(4,128)}, u32[]{:S(2)}) copy-start(f32[2,4,512]{2,1,0:T(4,128)} %get-tuple-element.111) | copy-start | bytes 49156
  138.7 3.2 %copy-start.7 = (f32[2,4,512]{2,1,0:T(4,128)S(1)}, f32[2,4,512]{2,1,0:T(4,128)}, u32[]{:S(2)}) copy-start(f32[2,4,512]{2,1,0:T(4,128)} %get-tuple-element.112) | copy-start | bytes 49156
  138.7 3.2 %copy-start.9 = (f32[2,512]{1,0:T(2,128)S(1)}, f32[2,512]{1,0:T(2,128)}, u32[]{:S(2)}) copy-start(f32[2,512]{1,0:T(2,128)} %sub.98) | copy-start | bytes 12292
  138.8 3.2 %copy-start.11 = (f32[2,512]{1,0:T(2,128)S(1)}, f32[2,512]{1,0:T(2,128)}, u32[]{:S(2)}) copy-start(f32[2,512]{1,0:T(2,128)} %sub.103) | copy-start | bytes 12292
  138.8 3.2 %copy-start.13 = (f32[2,512]{1,0:T(2,128)S(1)}, f32[2,512]{1,0:T(2,128)}, u32[]{:S(2)}) copy-start(f32[2,512]{1,0:T(2,128)} %sub.108) | copy-start | bytes 12292
  138.8 3.2 %copy-start.15 = (pred[2,4]{1,0:T(4,128)(4,1)S(1)}, pred[2,4]{1,0:T(4,128)(4,1)}, u32[]{:S(2)}) copy-start(pred[2,4]{1,0:T(4,128)(4,1)} %get-tuple-element.102) | copy-start | bytes 28
  188.0 7.6 %collective-permute-start.17 = (f32[2,64,256]{2,1,0:T(8,128)S(1)}, f32[2,64,256]{2,1,0:T(8,128)S(1)}, u32[]{:S(2)}, u32[]{:S(2)}) collective-permute-start(f32[2,64,256]{2,1,0:T(8,128)S(1)} %fusion.41), channel_id=1, source_target_pairs={{1,0},{2,1},{3,2},{4,3},{5,4},{6,5},{7,6},{8,7},{9,8},{10,9},{11,1... | collective-permute-start | bytes 393224 | tf_op jit(solution)/shard_map/ppermute | solution.py:15
  188.4 7.2 %collective-permute-start.16 = (f32[2,64,256]{2,1,0:T(8,128)S(1)}, f32[2,64,256]{2,1,0:T(8,128)}, u32[]{:S(2)}, u32[]{:S(2)}) collective-permute-start(f32[2,64,256]{2,1,0:T(8,128)S(1)} %fusion.41), channel_id=1, source_target_pairs={{31,0},{0,1},{1,2},{2,3},{3,4},{4,5},{5,6},{6,7},{7,8},{8,9},{9,10... | collective-permute-start | bytes 393224 | tf_op jit(solution)/shard_map/ppermute | solution.py:15
  190.9 100.3 %collective-permute-start.15 = (f32[64,1024]{1,0:T(8,128)}, f32[64,1024]{1,0:T(8,128)}, u32[]{:S(2)}, u32[]{:S(2)}) collective-permute-start(f32[64,1024]{1,0:T(8,128)} %broadcast_multiply_fusion), channel_id=1, source_target_pairs={{1,0},{2,1},{3,2},{4,3},{5,4},{6,5},{7,6},{8,7},{9,8},{10,9},{11,1... | collective-permute-start | bytes 786440 | tf_op jit(solution)/shard_map/ppermute | solution.py:15
  194.6 96.6 %collective-permute-start.14 = (f32[64,1024]{1,0:T(8,128)}, f32[64,1024]{1,0:T(8,128)}, u32[]{:S(2)}, u32[]{:S(2)}) collective-permute-start(f32[64,1024]{1,0:T(8,128)} %broadcast_multiply_fusion), channel_id=1, source_target_pairs={{31,0},{0,1},{1,2},{2,3},{3,4},{4,5},{5,6},{6,7},{7,8},{8,9},{9,10... | collective-permute-start | bytes 786440 | tf_op jit(solution)/shard_map/ppermute | solution.py:15
  209.9 4.4 %collective-permute-start.18 = (f32[32,256]{1,0:T(8,128)}, f32[32,256]{1,0:T(8,128)S(1)}, u32[]{:S(2)}, u32[]{:S(2)}) collective-permute-start(f32[32,256]{1,0:T(8,128)} %reduce-scatter.5.cloned.1.call-done), channel_id=1, source_target_pairs={{4,0},{6,2},{8,4},{10,6},{12,8},{14,10},{16,12},{18,14},{20,16},{2... | collective-permute-start | bytes 98312 | tf_op jit(solution)/shard_map/ppermute | solution.py:15
  210.7 29.8 %collective-permute-start.25 = (f32[32,256]{1,0:T(8,128)}, f32[32,256]{1,0:T(8,128)S(1)}, u32[]{:S(2)}, u32[]{:S(2)}) collective-permute-start(f32[32,256]{1,0:T(8,128)} %reduce-scatter.5.cloned.1.call-done), channel_id=1, source_target_pairs={{22,0},{24,2},{26,4},{28,6},{30,8},{0,10},{2,12},{4,14},{6,16},{8,... | collective-permute-start | bytes 98312 | tf_op jit(solution)/shard_map/ppermute | solution.py:15
  213.1 27.4 %collective-permute-start.24 = (f32[32,256]{1,0:T(8,128)}, f32[32,256]{1,0:T(8,128)S(1)}, u32[]{:S(2)}, u32[]{:S(2)}) collective-permute-start(f32[32,256]{1,0:T(8,128)} %reduce-scatter.5.cloned.1.call-done), channel_id=1, source_target_pairs={{24,0},{26,2},{28,4},{30,6},{0,8},{2,10},{4,12},{6,14},{8,16},{10,... | collective-permute-start | bytes 98312 | tf_op jit(solution)/shard_map/ppermute | solution.py:15
  214.3 6.6 %collective-permute-start.19 = (f32[32,256]{1,0:T(8,128)}, f32[32,256]{1,0:T(8,128)S(1)}, u32[]{:S(2)}, u32[]{:S(2)}) collective-permute-start(f32[32,256]{1,0:T(8,128)} %reduce-scatter.5.cloned.1.call-done), channel_id=1, source_target_pairs={{6,0},{8,2},{10,4},{12,6},{14,8},{16,10},{18,12},{20,14},{22,16},{... | collective-permute-start | bytes 98312 | tf_op jit(solution)/shard_map/ppermute | solution.py:15
  220.9 5.8 %collective-permute-start.20 = (f32[32,256]{1,0:T(8,128)}, f32[32,256]{1,0:T(8,128)S(1)}, u32[]{:S(2)}, u32[]{:S(2)}) collective-permute-start(f32[32,256]{1,0:T(8,128)} %reduce-scatter.5.cloned.1.call-done), channel_id=1, source_target_pairs={{8,0},{10,2},{12,4},{14,6},{16,8},{18,10},{20,12},{22,14},{24,16},... | collective-permute-start | bytes 98312 | tf_op jit(solution)/shard_map/ppermute | solution.py:15
  226.7 4.0 %collective-permute-start.21 = (f32[32,256]{1,0:T(8,128)}, f32[32,256]{1,0:T(8,128)S(1)}, u32[]{:S(2)}, u32[]{:S(2)}) collective-permute-start(f32[32,256]{1,0:T(8,128)} %reduce-scatter.5.cloned.1.call-done), channel_id=1, source_target_pairs={{10,0},{12,2},{14,4},{16,6},{18,8},{20,10},{22,12},{24,14},{26,16}... | collective-permute-start | bytes 98312 | tf_op jit(solution)/shard_map/ppermute | solution.py:15
  230.7 3.2 %collective-permute-start.22 = (f32[32,256]{1,0:T(8,128)}, f32[32,256]{1,0:T(8,128)S(1)}, u32[]{:S(2)}, u32[]{:S(2)}) collective-permute-start(f32[32,256]{1,0:T(8,128)} %reduce-scatter.5.cloned.1.call-done), channel_id=1, source_target_pairs={{28,0},{30,2},{0,4},{2,6},{4,8},{6,10},{8,12},{10,14},{12,16},{14,... | collective-permute-start | bytes 98312 | tf_op jit(solution)/shard_map/ppermute | solution.py:15
  233.9 6.6 %collective-permute-start.23 = (f32[32,256]{1,0:T(8,128)}, f32[32,256]{1,0:T(8,128)S(1)}, u32[]{:S(2)}, u32[]{:S(2)}) collective-permute-start(f32[32,256]{1,0:T(8,128)} %reduce-scatter.5.cloned.1.call-done), channel_id=1, source_target_pairs={{26,0},{28,2},{30,4},{0,6},{2,8},{4,10},{6,12},{8,14},{10,16},{12,... | collective-permute-start | bytes 98312 | tf_op jit(solution)/shard_map/ppermute | solution.py:15
  292.4 1.8 copy-start.6
  292.4 1.8 copy-start.8
  292.4 1.8 copy-start.10
  292.4 1.8 copy-start.12
  292.5 1.8 copy-start.14
  292.5 1.8 copy-start.16
  (1 other events, 0.6 us)
Sparse Core Ops, SparseCore 0:
  25.7 16.0 reduce-scatter.2
  195.8 14.0 reduce-scatter.4
